TPU v7x, 32 devices: a whole 2x2x4 slice. The times are simulated.
32 devices in a mesh: clips: 2 (over y), frame: 4 (over z), rows: 2 (over x), view: 2 (over core).
Axes of the slice: x: 2, y: 2, z: 4, core: 2. Of those that a mesh axis runs over, the one named last changes fastest.
Arguments:
- feats: bfloat16 [4, 4, 8, 480, 256], P(('clips', 'view'), 'frame', 'rows'), parts along dimension 0, may hold values from -8 to 8
- norm_gains: float32 [3, 256], replicated, may hold values from 0.6 to 10
- cross_qkv: bfloat16 [256, 768], replicated, may hold values from -0.45 to 0.45
- cross_out: bfloat16 [256, 256], replicated, may hold values from -0.375 to 0.375
- time_qkv: bfloat16 [256, 768], replicated, may hold values from -0.45 to 0.45
- time_out: bfloat16 [256, 256], replicated, may hold values from -0.375 to 0.375
- mlp_in: bfloat16 [256, 1024], replicated, may hold values from -0.375 to 0.375
- mlp_out: bfloat16 [1024, 256], replicated, may hold values from -0.1875 to 0.1875
Outputs:
- result: bfloat16 [4, 4, 8, 480, 256], P(('clips', 'view'), 'frame', 'rows'), parts along dimension 0
There are 2 independent parts, one for each index of `clips`. A program takes and returns all parts, laid end to end along the dimension named above; an argument that names none is the same for every part. Nothing has to cross between parts.
All inputs are finite; a program needn't handle non-finite values.
Results may differ from a plain program's by a relative error of at most 0.012.
Values may be sent and summed in bfloat16 or wider, within the bound.
No kernel may reach another device: no remote copies, remote signals or barrier semaphores. Data moves between devices by JAX's collectives and lax.ppermute only.
A program may use at most 64 MiB of HBM per device.

v0:
```python
import jax
import jax.numpy as jnp
from jax import lax
from jax.sharding import PartitionSpec as P

HEADS = 8
EPSILON = 1e-05


def swapped(value, axis, bit):
    return lax.ppermute(value, axis, [(i, i ^ 1 << bit) for i in range(lax.axis_size(axis))])


def layer_norm(values, norm_gain):
    wide = values.astype(jnp.float32)
    centre = jnp.mean(wide, axis=-1, keepdims=True)
    spread = jnp.mean((wide - centre) ** 2, axis=-1, keepdims=True)
    return ((wide - centre) * lax.rsqrt(spread + EPSILON) * norm_gain).astype(jnp.bfloat16)


def row_attend(queries, key_rows, value_rows):
    length, channels = queries.shape
    head_dim = channels // HEADS
    q_heads = queries.reshape(length, HEADS, head_dim)
    k_heads = key_rows.reshape(length, HEADS, head_dim)
    v_heads = value_rows.reshape(length, HEADS, head_dim)
    scores = jnp.einsum(
        "qhd,khd->hqk", q_heads, k_heads, preferred_element_type=jnp.float32
    ) * head_dim ** (-0.5)
    top_score = jnp.max(scores, axis=-1, keepdims=True)
    expo = jnp.exp(scores - top_score)
    shares = (expo / jnp.sum(expo, axis=-1, keepdims=True)).astype(jnp.bfloat16)
    mixed = jnp.einsum("hqk,khd->qhd", shares, v_heads, preferred_element_type=jnp.float32)
    return mixed.reshape(length, channels).astype(jnp.bfloat16)


def time_attend(queries, key_rows, value_rows):
    frames, pixels, channels = queries.shape
    head_dim = channels // HEADS
    q_heads = queries.reshape(frames, pixels, HEADS, head_dim)
    k_heads = key_rows.reshape(frames, pixels, HEADS, head_dim)
    v_heads = value_rows.reshape(frames, pixels, HEADS, head_dim)
    scores = jnp.einsum(
        "fnhd,gnhd->hfgn", q_heads, k_heads, preferred_element_type=jnp.float32
    ) * head_dim ** (-0.5)
    top_score = jnp.max(scores, axis=2, keepdims=True)
    expo = jnp.exp(scores - top_score)
    shares = (expo / jnp.sum(expo, axis=2, keepdims=True)).astype(jnp.bfloat16)
    mixed = jnp.einsum("hfgn,gnhd->fnhd", shares, v_heads, preferred_element_type=jnp.float32)
    return mixed.reshape(frames, pixels, channels).astype(jnp.bfloat16)


def local(feats, norm_gains, cross_qkv, cross_out, time_qkv, time_out, mlp_in, mlp_out):
    rows_here, row_width, channels = (feats.shape[2], feats.shape[3], feats.shape[4])
    frame_count = lax.axis_size("frame")
    tokens_flat = feats[0, 0].reshape(-1, channels)
    pixel_count = tokens_flat.shape[0]
    block_pixels = pixel_count // frame_count
    normed_a = layer_norm(tokens_flat, norm_gains[0])
    projected = jnp.dot(normed_a, cross_qkv, preferred_element_type=jnp.float32).astype(
        jnp.bfloat16
    )
    queries = projected[:, :channels]
    partner = swapped(projected[:, channels:], "view", 0)

    def cross_row(pieces):
        return row_attend(pieces[0], pieces[1][:, :channels], pieces[1][:, channels:])

    cross_mix = lax.map(
        cross_row,
        (
            queries.reshape(rows_here, row_width, channels),
            partner.reshape(rows_here, row_width, 2 * channels),
        ),
    )
    cross_mix = cross_mix.reshape(-1, channels)
    stream_b = (
        tokens_flat.astype(jnp.float32)
        + jnp.dot(cross_mix, cross_out, preferred_element_type=jnp.float32)
    ).astype(jnp.bfloat16)
    normed_b = layer_norm(stream_b, norm_gains[1])
    outgoing = normed_b.reshape(1, frame_count, block_pixels, channels)
    gathered = lax.all_to_all(outgoing, "frame", split_axis=1, concat_axis=0, tiled=True)[:, 0]
    frames, pixels, _ = gathered.shape
    projected_b = jnp.dot(
        gathered.reshape(-1, channels), time_qkv, preferred_element_type=jnp.float32
    ).astype(jnp.bfloat16)
    projected_b = projected_b.reshape(frames, pixels, 3 * channels)
    mixed = time_attend(
        projected_b[..., :channels],
        projected_b[..., channels : 2 * channels],
        projected_b[..., 2 * channels :],
    )
    time_mix = mixed[:, None]
    returned = lax.all_to_all(time_mix, "frame", split_axis=0, concat_axis=1, tiled=True).reshape(
        pixel_count, channels
    )
    stream_c = (
        stream_b.astype(jnp.float32)
        + jnp.dot(returned, time_out, preferred_element_type=jnp.float32)
    ).astype(jnp.bfloat16)
    normed_c = layer_norm(stream_c, norm_gains[2])
    inner_act = jax.nn.gelu(
        jnp.dot(normed_c, mlp_in, preferred_element_type=jnp.float32), approximate=True
    ).astype(jnp.bfloat16)
    result = (
        stream_c.astype(jnp.float32)
        + jnp.dot(inner_act, mlp_out, preferred_element_type=jnp.float32)
    ).astype(jnp.bfloat16)
    return result.reshape(1, 1, rows_here, row_width, channels)


def solution(mesh):
    placed = (P(("clips", "view"), "frame", "rows", None, None), P(), P(), P(), P(), P(), P(), P())
    return jax.shard_map(
        local,
        mesh=mesh,
        in_specs=placed,
        out_specs=P(("clips", "view"), "frame", "rows", None, None),
        check_vma=False,
    )
```

profile of v0, /device:TPU:0, one launch (start us, length us, event | category | flops | bytes accessed | tf_op | source)
XLA Modules:
  0.0 185.9 jit_solution(15738146926986763434)
XLA Ops:
  1.7 1.8 multiply_reduce_fusion.1
  4.5 1.8 fusion.42
  10.2 2.8 %collective-permute-done = bf16[1920,512]{1,0:T(8,128)(2,1)S(1)} collective-permute-done((bf16[1920,512]{1,0:T(8,128)(2,1)}, bf16[1920,512]{1,0:T(8,128)(2,1)S(1)}, u32[]{:S(2)}, u32[]{:S(2)}) %collective-permute-start) | collective-permute-done | bytes 1966112 | tf_op jit(solution)/shard_map/ppermute | solution.py:11
  14.3 48.6 %while.10 = (s32[]{:T(128)}, bf16[4,480,256]{2,1,0:T(8,128)(2,1)}, bf16[4,480,512]{2,1,0:T(8,128)(2,1)}, bf16[4,480,256]{2,1,0:T(8,128)(2,1)}, s32[]{:T(128)}) while((s32[]{:T(128)}, bf16[4,480,256]{2,1,0:T(8,128)(2,1)}, bf16[4,480,512]{2,1,0:T(8,128)(2,1)}, bf16[4,480,256]{2,1,0:T(8,128)(2,1)}, s32[]{:T(128)}) %tuple.39), condition=%wide.region_5.6_spmd, body=%wide.region_2.5_spmd.sunk | while | flops 245268960 | bytes 20675140 | solution.py:69
  16.8 4.8 %fusion.91 = (f32[8,480]{1,0:T(8,128)S(1)}, f32[8,480,480]{1,2,0:T(8,128)}) fusion(bf16[480,8,32]{0,2,1:T(8,128)(2,1)S(1)} %bitcast.83, bf16[480,8,32]{0,2,1:T(8,128)(2,1)S(1)} %bitcast.86), kind=kOutput, calls=%fused_computation.73.clone.1 | convolution fusion | flops 123494880 | bytes 7879680 | tf_op jit(solution)/shard_map/while/body/eval_jaxpr/sub | solution.py:31
  21.6 4.0 %fusion.92 = bf16[8,32,480]{2,1,0:T(8,128)(2,1)S(1)} fusion(bf16[480,8,32]{0,2,1:T(8,128)(2,1)S(1)} %bitcast.85, f32[8,480,480]{1,2,0:T(8,128)} %get-tuple-element.101, f32[8,480]{1,0:T(8,128)S(1)} %get-tuple-element.102), kind=kOutput, calls=%fused_computation.7.clone.1 | convolution fusion | flops 121774080 | bytes 7879680 | tf_op jit(solution)/shard_map/while/body/eval_jaxpr/hqk,khd->qhd/dot_general | solution.py:33
  28.9 4.8 %fusion.91 = (f32[8,480]{1,0:T(8,128)S(1)}, f32[8,480,480]{1,2,0:T(8,128)}) fusion(bf16[480,8,32]{0,2,1:T(8,128)(2,1)S(1)} %bitcast.83, bf16[480,8,32]{0,2,1:T(8,128)(2,1)S(1)} %bitcast.86), kind=kOutput, calls=%fused_computation.73.clone.1 | convolution fusion | flops 123494880 | bytes 7879680 | tf_op jit(solution)/shard_map/while/body/eval_jaxpr/sub | solution.py:31
  33.7 4.0 %fusion.92 = bf16[8,32,480]{2,1,0:T(8,128)(2,1)S(1)} fusion(bf16[480,8,32]{0,2,1:T(8,128)(2,1)S(1)} %bitcast.85, f32[8,480,480]{1,2,0:T(8,128)} %get-tuple-element.101, f32[8,480]{1,0:T(8,128)S(1)} %get-tuple-element.102), kind=kOutput, calls=%fused_computation.7.clone.1 | convolution fusion | flops 121774080 | bytes 7879680 | tf_op jit(solution)/shard_map/while/body/eval_jaxpr/hqk,khd->qhd/dot_general | solution.py:33
  41.1 4.8 %fusion.91 = (f32[8,480]{1,0:T(8,128)S(1)}, f32[8,480,480]{1,2,0:T(8,128)}) fusion(bf16[480,8,32]{0,2,1:T(8,128)(2,1)S(1)} %bitcast.83, bf16[480,8,32]{0,2,1:T(8,128)(2,1)S(1)} %bitcast.86), kind=kOutput, calls=%fused_computation.73.clone.1 | convolution fusion | flops 123494880 | bytes 7879680 | tf_op jit(solution)/shard_map/while/body/eval_jaxpr/sub | solution.py:31
  45.9 4.0 %fusion.92 = bf16[8,32,480]{2,1,0:T(8,128)(2,1)S(1)} fusion(bf16[480,8,32]{0,2,1:T(8,128)(2,1)S(1)} %bitcast.85, f32[8,480,480]{1,2,0:T(8,128)} %get-tuple-element.101, f32[8,480]{1,0:T(8,128)S(1)} %get-tuple-element.102), kind=kOutput, calls=%fused_computation.7.clone.1 | convolution fusion | flops 121774080 | bytes 7879680 | tf_op jit(solution)/shard_map/while/body/eval_jaxpr/hqk,khd->qhd/dot_general | solution.py:33
  53.2 4.8 %fusion.91 = (f32[8,480]{1,0:T(8,128)S(1)}, f32[8,480,480]{1,2,0:T(8,128)}) fusion(bf16[480,8,32]{0,2,1:T(8,128)(2,1)S(1)} %bitcast.83, bf16[480,8,32]{0,2,1:T(8,128)(2,1)S(1)} %bitcast.86), kind=kOutput, calls=%fused_computation.73.clone.1 | convolution fusion | flops 123494880 | bytes 7879680 | tf_op jit(solution)/shard_map/while/body/eval_jaxpr/sub | solution.py:31
  58.0 4.0 %fusion.92 = bf16[8,32,480]{2,1,0:T(8,128)(2,1)S(1)} fusion(bf16[480,8,32]{0,2,1:T(8,128)(2,1)S(1)} %bitcast.85, f32[8,480,480]{1,2,0:T(8,128)} %get-tuple-element.101, f32[8,480]{1,0:T(8,128)S(1)} %get-tuple-element.102), kind=kOutput, calls=%fused_computation.7.clone.1 | convolution fusion | flops 121774080 | bytes 7879680 | tf_op jit(solution)/shard_map/while/body/eval_jaxpr/hqk,khd->qhd/dot_general | solution.py:33
  62.9 1.8 convert_reduce_fusion.1
  65.9 30.7 %all_to_all.8 = bf16[1,4,480,256]{3,2,0,1:T(8,128)(2,1)S(1)} all-to-all(bf16[1,4,480,256]{3,2,0,1:T(8,128)(2,1)S(1)} %bitcast.92), channel_id=1, replica_groups=mesh['clips'=2,'frame'=4,'rows'=2,'view'=2] {'frame'}, dimensions={1} | all-to-all | bytes 1966080 | tf_op jit(solution)/shard_map/all_to_all | solution.py:83
  100.5 4.6 %copy.60 = bf16[4,480,8,32]{3,0,1,2:T(4,128)(2,1)} copy(bf16[4,480,8,32]{1,3,2,0:T(8,128)(2,1)S(1)} %bitcast.88) | data formatting | bytes 1966080 | tf_op jit(solution)/shard_map/reshape | solution.py:41
  106.5 4.5 %copy.61 = bf16[4,480,8,32]{3,0,1,2:T(4,128)(2,1)} copy(bf16[4,480,8,32]{1,3,2,0:T(8,128)(2,1)S(1)} %bitcast.89) | data formatting | bytes 1966080 | tf_op jit(solution)/shard_map/reshape | solution.py:40
  111.0 8.4 %fusion.61 = f32[8,480,4,4]{3,2,1,0:T(4,128)} fusion(bf16[4,480,8,32]{3,0,1,2:T(4,128)(2,1)} %copy.60, bf16[4,480,8,32]{3,0,1,2:T(4,128)(2,1)} %copy.61), kind=kOutput, calls=%fused_computation.76 | convolution fusion | flops 3932160 | bytes 2211840 | tf_op jit(solution)/shard_map/fnhd,gnhd->hfgn/dot_general | solution.py:43
  119.5 5.1 %copy.62 = f32[8,480,4,4]{1,0,2,3:T(8,128)S(1)} copy(f32[8,480,4,4]{3,2,1,0:T(4,128)} %fusion.61) | data formatting | bytes 491520 | tf_op jit(solution)/shard_map/fnhd,gnhd->hfgn/dot_general | solution.py:43
  124.7 7.4 %copy.64 = bf16[8,4,4,480]{2,1,0,3:T(4,128)(2,1)} copy(bf16[8,4,4,480]{3,0,2,1:T(8,128)(2,1)S(1)} %divide_convert_fusion.4) | data formatting | bytes 245760 | tf_op jit(solution)/shard_map/convert_element_type | solution.py:48
  132.7 4.7 %copy.63 = bf16[4,480,8,32]{3,0,2,1:T(4,128)(2,1)} copy(bf16[4,480,8,32]{1,3,2,0:T(8,128)(2,1)S(1)} %bitcast.90) | data formatting | bytes 1966080 | tf_op jit(solution)/shard_map/reshape | solution.py:42
  137.4 9.5 %fusion.20 = bf16[4,480,8,32]{3,0,2,1:T(4,128)(2,1)} fusion(bf16[4,480,8,32]{3,0,2,1:T(4,128)(2,1)} %copy.63, bf16[8,4,4,480]{2,1,0,3:T(4,128)(2,1)} %copy.64), kind=kOutput, calls=%fused_computation.24 | convolution fusion | flops 4423680 | bytes 2088960 | tf_op jit(solution)/shard_map/hfgn,gnhd->fnhd/dot_general | solution.py:49
  146.9 5.4 %copy.65 = bf16[4,480,8,32]{1,3,2,0:T(8,128)(2,1)S(1)} copy(bf16[4,480,8,32]{3,0,2,1:T(4,128)(2,1)} %fusion.20) | data formatting | bytes 1966080 | tf_op jit(solution)/shard_map/convert_element_type | solution.py:50
  152.9 26.7 %all_to_all.9 = bf16[4,1,480,256]{3,2,1,0:T(8,128)(2,1)S(1)} all-to-all(bf16[4,1,480,256]{3,2,1,0:T(8,128)(2,1)S(1)} %copy.66), channel_id=1, replica_groups=mesh['clips'=2,'frame'=4,'rows'=2,'view'=2] {'frame'}, dimensions={0} | all-to-all | bytes 1966080 | tf_op jit(solution)/shard_map/all_to_all | solution.py:95
  181.7 4.2 %fusion.27 = bf16[1920,256]{1,0:T(8,128)(2,1)} fusion(bf16[1024,256]{1,0:T(8,128)(2,1)S(1)} %copy-done, bf16[256,1024]{1,0:T(8,128)(2,1)S(1)} %copy-done.6, bf16[1920,256]{1,0:T(8,128)(2,1)S(1)} %get-tuple-element.69, f32[256]{0:T(256)S(1)} %bitcast.98, f32[1920]{0:T(1024)S(1)} %add_rsqrt_fusion, f32[1920]{0:T(1024)S(1)} %broadcast_multiply_fusion), kind=kOutput, calls=%fused_computation.37 | convolution fusion | flops 2034892800 | bytes 3031040 | tf_op jit(solution)/shard_map/dot_general | solution.py:108
  (70 shorter events, 31.0 us)
Async XLA Ops:
  0.0 181.7 %copy-start = (bf16[1024,256]{1,0:T(8,128)(2,1)S(1)}, bf16[1024,256]{1,0:T(8,128)(2,1)}, u32[]{:S(2)}) copy-start(bf16[1024,256]{1,0:T(8,128)(2,1)} %param.17) | copy-start | bytes 1572868
  0.0 6.2 %copy-start.3 = (bf16[256,768]{1,0:T(8,128)(2,1)S(1)}, bf16[256,768]{1,0:T(8,128)(2,1)}, u32[]{:S(2)}) copy-start(bf16[256,768]{1,0:T(8,128)(2,1)} %param.12) | copy-start | bytes 1179652
  8.6 4.3 %collective-permute-start = (bf16[1920,512]{1,0:T(8,128)(2,1)}, bf16[1920,512]{1,0:T(8,128)(2,1)S(1)}, u32[]{:S(2)}, u32[]{:S(2)}) collective-permute-start(bf16[1920,512]{1,0:T(8,128)(2,1)} %slice.40), channel_id=1, source_target_pairs={{0,1},{1,0},{2,3},{3,2},{4,5},{5,4},{6,7},{7,6},{8,9},{9,8},{10,11... | collective-permute-start | bytes 5898248 | tf_op jit(solution)/shard_map/ppermute | solution.py:11
  12.9 1.4 copy-start.2
  14.3 48.6 %copy-start.1 = (bf16[1,1,4,480,256]{4,3,2,1,0:T(8,128)(2,1)S(1)}, bf16[1,1,4,480,256]{4,3,2,1,0:T(8,128)(2,1)}, u32[]{:S(2)}) copy-start(bf16[1,1,4,480,256]{4,3,2,1,0:T(8,128)(2,1)} %param.10) | copy-start | bytes 2949124
  14.3 48.6 %copy-start.5 = (bf16[256,256]{1,0:T(8,128)(2,1)S(1)}, bf16[256,256]{1,0:T(8,128)(2,1)}, u32[]{:S(2)}) copy-start(bf16[256,256]{1,0:T(8,128)(2,1)} %param.13) | copy-start | bytes 393220
  62.9 33.7 %copy-start.4 = (bf16[256,768]{1,0:T(8,128)(2,1)S(1)}, bf16[256,768]{1,0:T(8,128)(2,1)}, u32[]{:S(2)}) copy-start(bf16[256,768]{1,0:T(8,128)(2,1)} %param.14) | copy-start | bytes 1179652
  179.6 2.1 %copy-start.6 = (bf16[256,1024]{1,0:T(8,128)(2,1)S(1)}, bf16[256,1024]{1,0:T(8,128)(2,1)}, u32[]{:S(2)}) copy-start(bf16[256,1024]{1,0:T(8,128)(2,1)} %param.16) | copy-start | bytes 1572868
where the time goes:
time: 187 us; the launch traced here: 186 us
  matrix products  62.5 us (33%)
  blocking collectives  57.4 us (31%)
  local copies, waits for them, and re-layouts  55.2 us (30%)
  other arithmetic  7.24 us (4%)
  waiting for transfers between devices  2.78 us (1%)
    all_to_all x1, blocking collectives, local(): lax.all_to_all(outgoing, 'frame', split_axis=1, concat_axis=0, tiled=True)  30.7 us
    all_to_all x1, blocking collectives, local(): lax.all_to_all(time_mix, 'frame', split_axis=0, concat_axis=1, tiled=True)  26.7 us
    sub x4, matrix products, row_attend(): expo = jnp.exp(scores - top_score)  19.1 us
    dot_general x4, matrix products, row_attend(): jnp.einsum('hqk,khd->qhd', shares, v_heads, preferred_element_type=jnp.fl...  16.1 us
    dynamic_slice x16, local copies, waits for them, and re-layouts, local(): lax.map(cross_row, (queries.reshape(rows_here, row_width, channels), part...  9.61 us
    dot_general x1, matrix products, time_attend(): jnp.einsum('hfgn,gnhd->fnhd', shares, v_heads, preferred_element_type=jnp...  9.5 us
    dot_general x1, matrix products, time_attend(): jnp.einsum('fnhd,gnhd->hfgn', q_heads, k_heads, preferred_element_type=jn...  8.41 us
    convert_element_type x1, local copies, waits for them, and re-layouts, time_attend(): shares = (expo / jnp.sum(expo, axis=2, keepdims=True)).astype(jnp.bfloat16)  7.42 us
  transfers between devices with their start and end apart: 1, of which 1 were waited for; matrix products, arithmetic and copies ran while one was open for 1% of the time, Pallas kernels for 0%

commit v1 on v0

--- a/solution.py
+++ b/solution.py
@@ -2,6 +2,7 @@
 import jax.numpy as jnp
 from jax import lax
 from jax.sharding import PartitionSpec as P
+from jax.lax import all_to_all, psum
 
 HEADS = 8
 EPSILON = 1e-05
@@ -92,9 +93,15 @@
         projected_b[..., 2 * channels :],
     )
     time_mix = mixed[:, None]
-    returned = lax.all_to_all(time_mix, "frame", split_axis=0, concat_axis=1, tiled=True).reshape(
-        pixel_count, channels
-    )
+    returned = jnp.concatenate(
+        all_to_all(
+            jnp.stack(jnp.split(time_mix, psum(1, axis_name="frame"), axis=0), axis=0),
+            axis_name="frame",
+            split_axis=0,
+            concat_axis=0,
+        ),
+        axis=1,
+    ).reshape(pixel_count, channels)
     stream_c = (
         stream_b.astype(jnp.float32)
         + jnp.dot(returned, time_out, preferred_element_type=jnp.float32)

time: 187 us -> 215 us (1.15)
  local copies, waits for them, and re-layouts: 55.2 us -> 82.4 us
    split x0 -> x5, local copies, waits for them, and re-layouts: none -> 32.6 us  [local(): jnp.split(time_mix, psum(1, axis_name='frame'), axis=0)]
    convert_element_type x2 -> x0, local copies, waits for them, and re-layouts: 5.96 us -> none  [time_attend(): return mixed.reshape(frames, pixels, channels).astype(jnp.bfloat16)]
  transfers between devices with their start and end apart: 1 -> 1, of which waited for: 1 -> 1; matrix products, arithmetic and copies ran while one was open for 1% -> 0% of each run, Pallas kernels for 0% -> 0%
where the time goes in v1:
time: 215 us; the launch traced here: 214 us
  local copies, waits for them, and re-layouts  82.4 us (38%)
  matrix products  62.2 us (29%)
  blocking collectives  57.5 us (27%)
  other arithmetic  8.35 us (4%)
  waiting for transfers between devices  2.78 us (1%)
    split x5, local copies, waits for them, and re-layouts, local(): jnp.split(time_mix, psum(1, axis_name='frame'), axis=0)  32.6 us
    all_to_all x1, blocking collectives, local(): lax.all_to_all(outgoing, 'frame', split_axis=1, concat_axis=0, tiled=True)  30.7 us
    all_to_all x1, blocking collectives, local(): all_to_all(jnp.stack(jnp.split(time_mix, psum(1, axis_name='frame'), axis...  26.9 us
    sub x4, matrix products, row_attend(): expo = jnp.exp(scores - top_score)  19.1 us
    dot_general x4, matrix products, row_attend(): jnp.einsum('hqk,khd->qhd', shares, v_heads, preferred_element_type=jnp.fl...  16.1 us
    dynamic_slice x16, local copies, waits for them, and re-layouts, local(): lax.map(cross_row, (queries.reshape(rows_here, row_width, channels), part...  9.61 us
    dot_general x1, matrix products, time_attend(): jnp.einsum('hfgn,gnhd->fnhd', shares, v_heads, preferred_element_type=jnp...  9.4 us
    dot_general x1, matrix products, time_attend(): jnp.einsum('fnhd,gnhd->hfgn', q_heads, k_heads, preferred_element_type=jn...  8.41 us
  transfers between devices with their start and end apart: 1, of which 1 were waited for; matrix products, arithmetic and copies ran while one was open for 0% of the time, Pallas kernels for 0%

profile of v1, /device:TPU:0, one launch (start us, length us, event | category | flops | bytes accessed | tf_op | source)
XLA Modules:
  0.0 214.1 jit_solution(3277085998214773750)
XLA Ops:
  14.3 48.6 %while.10 = (s32[]{:T(128)}, bf16[4,480,256]{2,1,0:T(8,128)(2,1)}, bf16[4,480,512]{2,1,0:T(8,128)(2,1)}, bf16[4,480,256]{2,1,0:T(8,128)(2,1)}, s32[]{:T(128)}) while((s32[]{:T(128)}, bf16[4,480,256]{2,1,0:T(8,128)(2,1)}, bf16[4,480,512]{2,1,0:T(8,128)(2,1)}, bf16[4,480,256]{2,1,0:T(8,128)(2,1)}, s32[]{:T(128)}) %tuple.42), condition=%wide.region_5.6_spmd, body=%wide.region_2.5_spmd.sunk | while | flops 245268960 | bytes 20675140 | solution.py:70
  16.8 4.8 %fusion.92 = (f32[8,480]{1,0:T(8,128)S(1)}, f32[8,480,480]{1,2,0:T(8,128)}) fusion(bf16[480,8,32]{0,2,1:T(8,128)(2,1)S(1)} %bitcast.86, bf16[480,8,32]{0,2,1:T(8,128)(2,1)S(1)} %bitcast.89), kind=kOutput, calls=%fused_computation.74.clone.1 | convolution fusion | flops 123494880 | bytes 7879680 | tf_op jit(solution)/shard_map/while/body/eval_jaxpr/sub | solution.py:32
  21.6 4.0 %fusion.93 = bf16[8,32,480]{2,1,0:T(8,128)(2,1)S(1)} fusion(bf16[480,8,32]{0,2,1:T(8,128)(2,1)S(1)} %bitcast.88, f32[8,480,480]{1,2,0:T(8,128)} %get-tuple-element.105, f32[8,480]{1,0:T(8,128)S(1)} %get-tuple-element.106), kind=kOutput, calls=%fused_computation.7.clone.1 | convolution fusion | flops 121774080 | bytes 7879680 | tf_op jit(solution)/shard_map/while/body/eval_jaxpr/hqk,khd->qhd/dot_general | solution.py:34
  28.9 4.8 %fusion.92 = (f32[8,480]{1,0:T(8,128)S(1)}, f32[8,480,480]{1,2,0:T(8,128)}) fusion(bf16[480,8,32]{0,2,1:T(8,128)(2,1)S(1)} %bitcast.86, bf16[480,8,32]{0,2,1:T(8,128)(2,1)S(1)} %bitcast.89), kind=kOutput, calls=%fused_computation.74.clone.1 | convolution fusion | flops 123494880 | bytes 7879680 | tf_op jit(solution)/shard_map/while/body/eval_jaxpr/sub | solution.py:32
  33.7 4.0 %fusion.93 = bf16[8,32,480]{2,1,0:T(8,128)(2,1)S(1)} fusion(bf16[480,8,32]{0,2,1:T(8,128)(2,1)S(1)} %bitcast.88, f32[8,480,480]{1,2,0:T(8,128)} %get-tuple-element.105, f32[8,480]{1,0:T(8,128)S(1)} %get-tuple-element.106), kind=kOutput, calls=%fused_computation.7.clone.1 | convolution fusion | flops 121774080 | bytes 7879680 | tf_op jit(solution)/shard_map/while/body/eval_jaxpr/hqk,khd->qhd/dot_general | solution.py:34
  41.1 4.8 %fusion.92 = (f32[8,480]{1,0:T(8,128)S(1)}, f32[8,480,480]{1,2,0:T(8,128)}) fusion(bf16[480,8,32]{0,2,1:T(8,128)(2,1)S(1)} %bitcast.86, bf16[480,8,32]{0,2,1:T(8,128)(2,1)S(1)} %bitcast.89), kind=kOutput, calls=%fused_computation.74.clone.1 | convolution fusion | flops 123494880 | bytes 7879680 | tf_op jit(solution)/shard_map/while/body/eval_jaxpr/sub | solution.py:32
  45.9 4.0 %fusion.93 = bf16[8,32,480]{2,1,0:T(8,128)(2,1)S(1)} fusion(bf16[480,8,32]{0,2,1:T(8,128)(2,1)S(1)} %bitcast.88, f32[8,480,480]{1,2,0:T(8,128)} %get-tuple-element.105, f32[8,480]{1,0:T(8,128)S(1)} %get-tuple-element.106), kind=kOutput, calls=%fused_computation.7.clone.1 | convolution fusion | flops 121774080 | bytes 7879680 | tf_op jit(solution)/shard_map/while/body/eval_jaxpr/hqk,khd->qhd/dot_general | solution.py:34
  53.2 4.8 %fusion.92 = (f32[8,480]{1,0:T(8,128)S(1)}, f32[8,480,480]{1,2,0:T(8,128)}) fusion(bf16[480,8,32]{0,2,1:T(8,128)(2,1)S(1)} %bitcast.86, bf16[480,8,32]{0,2,1:T(8,128)(2,1)S(1)} %bitcast.89), kind=kOutput, calls=%fused_computation.74.clone.1 | convolution fusion | flops 123494880 | bytes 7879680 | tf_op jit(solution)/shard_map/while/body/eval_jaxpr/sub | solution.py:32
  58.0 4.0 %fusion.93 = bf16[8,32,480]{2,1,0:T(8,128)(2,1)S(1)} fusion(bf16[480,8,32]{0,2,1:T(8,128)(2,1)S(1)} %bitcast.88, f32[8,480,480]{1,2,0:T(8,128)} %get-tuple-element.105, f32[8,480]{1,0:T(8,128)S(1)} %get-tuple-element.106), kind=kOutput, calls=%fused_computation.7.clone.1 | convolution fusion | flops 121774080 | bytes 7879680 | tf_op jit(solution)/shard_map/while/body/eval_jaxpr/hqk,khd->qhd/dot_general | solution.py:34
  65.8 30.7 %all_to_all.14 = bf16[1,4,480,256]{3,2,0,1:T(8,128)(2,1)S(1)} all-to-all(bf16[1,4,480,256]{3,2,0,1:T(8,128)(2,1)S(1)} %bitcast.94), channel_id=1, replica_groups=mesh['clips'=2,'frame'=4,'rows'=2,'view'=2] {'frame'}, dimensions={1} | all-to-all | bytes 1966080 | tf_op jit(solution)/shard_map/all_to_all | solution.py:84
  100.5 4.6 %copy.69 = bf16[4,480,8,32]{3,0,1,2:T(4,128)(2,1)} copy(bf16[4,480,8,32]{1,3,2,0:T(8,128)(2,1)S(1)} %bitcast.91) | data formatting | bytes 1966080 | tf_op jit(solution)/shard_map/reshape | solution.py:42
  105.6 4.5 %copy.70 = bf16[4,480,8,32]{3,0,1,2:T(4,128)(2,1)} copy(bf16[4,480,8,32]{1,3,2,0:T(8,128)(2,1)S(1)} %bitcast.92) | data formatting | bytes 1966080 | tf_op jit(solution)/shard_map/reshape | solution.py:41
  110.1 8.4 %fusion.62 = f32[8,480,4,4]{3,2,1,0:T(4,128)} fusion(bf16[4,480,8,32]{3,0,1,2:T(4,128)(2,1)} %copy.69, bf16[4,480,8,32]{3,0,1,2:T(4,128)(2,1)} %copy.70), kind=kOutput, calls=%fused_computation.78 | convolution fusion | flops 3932160 | bytes 2211840 | tf_op jit(solution)/shard_map/fnhd,gnhd->hfgn/dot_general | solution.py:44
  118.5 5.1 %copy.71 = f32[8,480,4,4]{1,0,2,3:T(8,128)S(1)} copy(f32[8,480,4,4]{3,2,1,0:T(4,128)} %fusion.62) | data formatting | bytes 491520 | tf_op jit(solution)/shard_map/fnhd,gnhd->hfgn/dot_general | solution.py:44
  123.7 7.4 %copy.73 = bf16[8,4,4,480]{2,1,0,3:T(4,128)(2,1)} copy(bf16[8,4,4,480]{3,0,2,1:T(8,128)(2,1)S(1)} %divide_convert_fusion.4) | data formatting | bytes 245760 | tf_op jit(solution)/shard_map/convert_element_type | solution.py:49
  132.6 4.7 %copy.72 = bf16[4,480,8,32]{3,0,2,1:T(4,128)(2,1)} copy(bf16[4,480,8,32]{1,3,2,0:T(8,128)(2,1)S(1)} %bitcast.93) | data formatting | bytes 1966080 | tf_op jit(solution)/shard_map/reshape | solution.py:43
  137.3 9.4 %fusion.20 = bf16[4,480,8,32]{3,0,2,1:T(4,128)(2,1)} fusion(bf16[4,480,8,32]{3,0,2,1:T(4,128)(2,1)} %copy.72, bf16[8,4,4,480]{2,1,0,3:T(4,128)(2,1)} %copy.73), kind=kOutput, calls=%fused_computation.24 | convolution fusion | flops 4423680 | bytes 2088960 | tf_op jit(solution)/shard_map/hfgn,gnhd->fnhd/dot_general | solution.py:50
  146.7 13.9 %fusion.59 = (bf16[1,480,8,32]{3,0,2,1:T(2,128)(2,1)}, bf16[1,480,8,32]{3,0,2,1:T(2,128)(2,1)}, bf16[1,480,8,32]{3,0,2,1:T(2,128)(2,1)}, bf16[1,480,8,32]{3,0,2,1:T(2,128)(2,1)}) fusion(bf16[4,480,8,32]{3,0,2,1:T(4,128)(2,1)} %fusion.20), kind=kLoop, calls=%fused_computation.75 | loop fusion | bytes 1966080 | tf_op jit(solution)/shard_map/split | solution.py:98
  160.6 4.4 %copy.74 = bf16[1,480,8,32]{1,3,2,0:T(8,128)(2,1)S(1)} copy(bf16[1,480,8,32]{3,0,2,1:T(2,128)(2,1)} %get-tuple-element.60) | data formatting | bytes 491520 | tf_op jit(solution)/shard_map/split | solution.py:98
  165.0 4.4 %copy.75 = bf16[1,480,8,32]{1,3,2,0:T(8,128)(2,1)S(1)} copy(bf16[1,480,8,32]{3,0,2,1:T(2,128)(2,1)} %get-tuple-element.63) | data formatting | bytes 491520 | tf_op jit(solution)/shard_map/split | solution.py:98
  169.4 4.4 %copy.76 = bf16[1,480,8,32]{1,3,2,0:T(8,128)(2,1)S(1)} copy(bf16[1,480,8,32]{3,0,2,1:T(2,128)(2,1)} %get-tuple-element.62) | data formatting | bytes 491520 | tf_op jit(solution)/shard_map/split | solution.py:98
  173.8 5.5 %copy.77 = bf16[1,480,8,32]{1,3,2,0:T(8,128)(2,1)} copy(bf16[1,480,8,32]{3,0,2,1:T(2,128)(2,1)} %get-tuple-element.61) | data formatting | bytes 491520 | tf_op jit(solution)/shard_map/split | solution.py:98
  181.0 26.9 %all_to_all.15 = bf16[4,1,1,480,256]{4,3,2,1,0:T(8,128)(2,1)S(1)} all-to-all(bf16[4,1,1,480,256]{4,3,2,1,0:T(8,128)(2,1)S(1)} %copy.78), channel_id=1, replica_groups=mesh['clips'=2,'frame'=4,'rows'=2,'view'=2] {'frame'}, dimensions={0} | all-to-all | bytes 1966080 | tf_op jit(solution)/shard_map/all_to_all | solution.py:97
  210.0 4.2 %fusion.27 = bf16[1920,256]{1,0:T(8,128)(2,1)} fusion(bf16[1024,256]{1,0:T(8,128)(2,1)S(1)} %copy-done, bf16[256,1024]{1,0:T(8,128)(2,1)S(1)} %copy-done.6, bf16[1920,256]{1,0:T(8,128)(2,1)S(1)} %get-tuple-element.73, f32[256]{0:T(256)S(1)} %bitcast.104, f32[1920]{0:T(1024)S(1)} %add_rsqrt_fusion, f32[1920]{0:T(1024)S(1)} %broadcast_multiply_fusion), kind=kOutput, calls=%fused_computation.37 | convolution fusion | flops 2034892800 | bytes 3031040 | tf_op jit(solution)/shard_map/dot_general | solution.py:115
  (75 shorter events, 40.2 us)
Async XLA Ops:
  0.0 209.9 %copy-start = (bf16[1024,256]{1,0:T(8,128)(2,1)S(1)}, bf16[1024,256]{1,0:T(8,128)(2,1)}, u32[]{:S(2)}) copy-start(bf16[1024,256]{1,0:T(8,128)(2,1)} %param.17) | copy-start | bytes 1572868
  0.0 6.2 %copy-start.3 = (bf16[256,768]{1,0:T(8,128)(2,1)S(1)}, bf16[256,768]{1,0:T(8,128)(2,1)}, u32[]{:S(2)}) copy-start(bf16[256,768]{1,0:T(8,128)(2,1)} %param.12) | copy-start | bytes 1179652
  8.6 4.3 %collective-permute-start = (bf16[1920,512]{1,0:T(8,128)(2,1)}, bf16[1920,512]{1,0:T(8,128)(2,1)S(1)}, u32[]{:S(2)}, u32[]{:S(2)}) collective-permute-start(bf16[1920,512]{1,0:T(8,128)(2,1)} %slice.48), channel_id=1, source_target_pairs={{0,1},{1,0},{2,3},{3,2},{4,5},{5,4},{6,7},{7,6},{8,9},{9,8},{10,11... | collective-permute-start | bytes 5898248 | tf_op jit(solution)/shard_map/ppermute | solution.py:12
  12.9 1.4 copy-start.2
  14.3 48.6 %copy-start.1 = (bf16[1,1,4,480,256]{4,3,2,1,0:T(8,128)(2,1)S(1)}, bf16[1,1,4,480,256]{4,3,2,1,0:T(8,128)(2,1)}, u32[]{:S(2)}) copy-start(bf16[1,1,4,480,256]{4,3,2,1,0:T(8,128)(2,1)} %param.10) | copy-start | bytes 2949124
  14.3 48.6 %copy-start.5 = (bf16[256,256]{1,0:T(8,128)(2,1)S(1)}, bf16[256,256]{1,0:T(8,128)(2,1)}, u32[]{:S(2)}) copy-start(bf16[256,256]{1,0:T(8,128)(2,1)} %param.13) | copy-start | bytes 393220
  64.6 31.9 %copy-start.4 = (bf16[256,768]{1,0:T(8,128)(2,1)S(1)}, bf16[256,768]{1,0:T(8,128)(2,1)}, u32[]{:S(2)}) copy-start(bf16[256,768]{1,0:T(8,128)(2,1)} %param.14) | copy-start | bytes 1179652
  181.0 29.0 %copy-start.6 = (bf16[256,1024]{1,0:T(8,128)(2,1)S(1)}, bf16[256,1024]{1,0:T(8,128)(2,1)}, u32[]{:S(2)}) copy-start(bf16[256,1024]{1,0:T(8,128)(2,1)} %param.16) | copy-start | bytes 1572868
